TPU v7x, 256 devices: a whole 4x4x8 slice. The times are simulated.
256 devices in a mesh: row: 8 (over x, core), col: 4 (over z_lo), layer: 8 (over y, z_hi).
Axes of the slice: x: 4, y: 4, z: 8 (z_hi: 2, z_lo: 4; z = z_hi * 4 + z_lo), core: 2. Of those that a mesh axis runs over, the one named last changes fastest.
Arguments:
- a_tiles: bfloat16 [8192, 16384], P('row', ('layer', 'col')), may hold values from -6 to 6
- a_occupancy: int32 [64, 128], P('row', ('layer', 'col')), may hold values 0 or 1
- b_tiles: bfloat16 [16384, 8192], P(('layer', 'row'), 'col'), may hold values from -0.046875 to 0.046875
- b_occupancy: int32 [128, 64], P(('layer', 'row'), 'col'), may hold values 0 or 1
Outputs:
- product: float32 [8192, 8192], P(('row', 'layer'), 'col')
Inputs may be any that keep to these rules, and one draw needn't show every extreme that they name: `a_occupancy`: each entry is 0 (block absent) or 1 (block present). `b_occupancy`: each entry is 0 (block absent) or 1 (block present).
All inputs are finite; a program needn't handle non-finite values.
Results may differ from a plain program's by a relative error of at most 0.0003.
Values may be sent and summed in bfloat16 or wider, within the bound.
A program may use at most 64 MiB of HBM per device.

v0:
```python
import jax
import jax.numpy as jnp
from jax import lax
from jax.sharding import PartitionSpec as P

BLOCK = 128


def keep_blocks(values, occupancy):
    height, breadth = values.shape
    tiled = values.reshape(height // BLOCK, BLOCK, breadth // BLOCK, BLOCK)
    flags = occupancy.astype(values.dtype)
    return (tiled * flags[:, None, :, None]).reshape(height, breadth)


def per_device(a_tiles, a_occupancy, b_tiles, b_occupancy):
    a_kept = keep_blocks(a_tiles, a_occupancy)
    b_kept = keep_blocks(b_tiles, b_occupancy)
    b_slab = lax.all_gather(b_kept, "row", axis=0, tiled=True)
    partial_value = jnp.dot(
        lax.all_gather(a_kept, "col", axis=1, tiled=True),
        b_slab,
        preferred_element_type=jnp.float32,
    )
    return lax.psum_scatter(partial_value, "layer", scatter_dimension=0, tiled=True)


def solution(mesh):
    in_specs = (
        P("row", ("layer", "col")),
        P("row", ("layer", "col")),
        P(("layer", "row"), "col"),
        P(("layer", "row"), "col"),
    )
    out_specs = P(("row", "layer"), "col")
    return jax.shard_map(
        per_device, mesh=mesh, in_specs=in_specs, out_specs=out_specs, check_vma=False
    )
```

profile of v0, /device:TPU:32, one launch (start us, length us, event | category | flops | bytes accessed | tf_op | source)
XLA Modules:
  0.0 355.3 jit_solution(10024609637868433303)
XLA Ops:
  6.5 0.0 all-gather.3.cloned.1.call-start
  6.5 0.7 convert_element_type.6
  7.2 0.1 copy.5
  7.3 0.3 mul.22
  7.7 2.3 bitcast_multiply_fusion.1
  10.0 0.0 all-gather.3.cloned.1.call-update
  10.0 0.0 all-gather.5.cloned.1.call-start
  10.1 0.7 convert_element_type.7
  10.8 0.2 mul.25
  11.0 2.5 bitcast_multiply_fusion
  13.5 0.0 all-gather.5.cloned.1.call-update
  13.5 0.0 reduce-scatter.2.cloned.1.call-start
  13.6 83.1 %all-gather.3.cloned.1.call-done = bf16[1024,2048]{1,0:T(8,128)(2,1)} async-done(((bf16[1024,512]{1,0:T(8,128)(2,1)}), bf16[1024,2048]{1,0:T(8,128)(2,1)}) %all-gather.3.cloned.1.call-update) | async-done | bytes 4194320 | tf_op jit(solution)/shard_map/all_gather | solution.py:21
  96.7 54.2 %all-gather.5.cloned.1.call-done = bf16[2048,2048]{1,0:T(8,128)(2,1)} async-done(((bf16[256,2048]{1,0:T(8,128)(2,1)}), bf16[2048,2048]{1,0:T(8,128)(2,1)}) %all-gather.5.cloned.1.call-update) | async-done | bytes 8388624 | tf_op jit(solution)/shard_map/all_gather | solution.py:19
  150.9 14.5 %fusion = f32[1024,2048]{1,0:T(8,128)} fusion(bf16[1024,2048]{1,0:T(8,128)(2,1)} %all-gather.3.cloned.1.call-done, bf16[2048,2048]{1,0:T(8,128)(2,1)} %all-gather.5.cloned.1.call-done), kind=kOutput, calls=%fused_computation.2 | convolution fusion | flops 8589934592 | bytes 20971520 | tf_op jit(solution)/shard_map/dot_general | solution.py:20
  165.4 0.0 reduce-scatter.2.cloned.1.call-update
  165.5 183.3 %reduce-scatter.2.cloned.1.call-done = f32[128,2048]{1,0:T(8,128)} async-done(((f32[1024,2048]{1,0:T(8,128)}), f32[128,2048]{1,0:T(8,128)}) %reduce-scatter.2.cloned.1.call-update) | async-done | bytes 1048592 | tf_op jit(solution)/shard_map/reduce_scatter | solution.py:25
Async XLA Ops:
  6.5 90.2 %all-gather.3.cloned.1.call-start = ((), (), s32[]{:S(2)}) async-start(), calls=%async_computation.1 | async-start | bytes 5242880 | tf_op jit(solution)/shard_map/all_gather | solution.py:21
  10.0 140.9 %all-gather.5.cloned.1.call-start = ((), (), s32[]{:S(2)}) async-start(), calls=%async_computation.2 | async-start | bytes 9437184 | tf_op jit(solution)/shard_map/all_gather | solution.py:19
  13.5 335.2 %reduce-scatter.2.cloned.1.call-start = ((), (), s32[]{:S(2)}) async-start(), calls=%async_computation.3 | async-start | bytes 9437184 | tf_op jit(solution)/shard_map/reduce_scatter | solution.py:25
Sparse Core Ops, SparseCore 0:
  10.2 86.4 all-gather.2
  98.6 52.3 all-gather.4
  165.6 183.1 reduce-scatter.1
where the time goes:
time: 355 us
  waiting for transfers between devices  321 us (90%)
  matrix products  14.5 us (4%)
  between operations  13.1 us (4%)
  other arithmetic  6.23 us (2%)
    reduce_scatter x1, waiting for transfers between devices, per_device(): lax.psum_scatter(partial_value, 'layer', scatter_dimension=0, tiled=True)  183 us
    all_gather x1, waiting for transfers between devices, per_device(): lax.all_gather(a_kept, 'col', axis=1, tiled=True)  83.1 us
    all_gather x1, waiting for transfers between devices, per_device(): b_slab = lax.all_gather(b_kept, 'row', axis=0, tiled=True)  54.2 us
    dot_general x1, matrix products, per_device(): jnp.dot(lax.all_gather(a_kept, 'col', axis=1, tiled=True), b_slab, prefer...  14.5 us
  transfers between devices with their start and end apart: 3, of which 3 were waited for; matrix products, arithmetic and copies ran while one was open for 1% of the time, Pallas kernels for 0%

commit v1 on v0

--- a/solution.py
+++ b/solution.py
@@ -16,7 +16,8 @@
 def per_device(a_tiles, a_occupancy, b_tiles, b_occupancy):
     a_kept = keep_blocks(a_tiles, a_occupancy)
     b_kept = keep_blocks(b_tiles, b_occupancy)
-    b_slab = lax.all_gather(b_kept, "row", axis=0, tiled=True)
+    repeated = jnp.stack([b_kept] * lax.axis_size("row"))
+    b_slab = jnp.concatenate(lax.all_to_all(repeated, "row", 0, 0), axis=0)
     partial_value = jnp.dot(
         lax.all_gather(a_kept, "col", axis=1, tiled=True),
         b_slab,

time: 355 us -> 318 us (0.90)
  waiting for transfers between devices: 321 us -> 276 us
  starting transfers between devices: 0.09 us -> 5.15 us
  local copies, waits for them, and re-layouts: 0.64 us -> 4.93 us
    all_gather x1 -> x0, waiting for transfers between devices: 54.2 us -> none  [per_device(): b_slab = lax.all_gather(b_kept, 'row', axis=0, tiled=True)]
    all_to_all x0 -> x1, starting transfers between devices: none -> 5.07 us  [per_device(): b_slab = jnp.concatenate(lax.all_to_all(repeated, 'row', 0, 0), axis=0)]
    all_to_all x0 -> x1, waiting for transfers between devices: none -> 5.04 us  [per_device(): b_slab = jnp.concatenate(lax.all_to_all(repeated, 'row', 0, 0), axis=0)]
    all_gather x1, waiting for transfers between devices: 83.1 us -> 87.8 us  [per_device(): lax.all_gather(a_kept, 'col', axis=1, tiled=True)]
    another operation x0 -> x1, local copies, waits for them, and re-layouts: none -> 4.28 us  [per_device(): repeated = jnp.stack([b_kept] * lax.axis_size('row'))]
  transfers between devices with their start and end apart: 3 -> 3, of which waited for: 3 -> 3; matrix products, arithmetic and copies ran while one was open for 1% -> 0% of each run, Pallas kernels for 0% -> 0%
where the time goes in v1:
time: 318 us; the launch traced here: 317 us
  waiting for transfers between devices  276 us (87%)
  matrix products  14.4 us (5%)
  between operations  13.5 us (4%)
  starting transfers between devices  5.15 us (2%)
  local copies, waits for them, and re-layouts  4.93 us (2%)
  other arithmetic  3.28 us (1%)
    reduce_scatter x1, waiting for transfers between devices, per_device(): lax.psum_scatter(partial_value, 'layer', scatter_dimension=0, tiled=True)  183 us
    all_gather x1, waiting for transfers between devices, per_device(): lax.all_gather(a_kept, 'col', axis=1, tiled=True)  87.8 us
    dot_general x1, matrix products, per_device(): jnp.dot(lax.all_gather(a_kept, 'col', axis=1, tiled=True), b_slab, prefer...  14.4 us
  transfers between devices with their start and end apart: 3, of which 3 were waited for; matrix products, arithmetic and copies ran while one was open for 0% of the time, Pallas kernels for 0%

profile of v1, /device:TPU:32, one launch (start us, length us, event | category | flops | bytes accessed | tf_op | source)
XLA Modules:
  0.0 317.3 jit_solution(12663031770164171315)
XLA Ops:
  6.5 0.7 convert_element_type.7
  7.2 0.2 mul.26
  7.4 1.5 bitcast_multiply_fusion
  8.9 4.3 %stack.3 = bf16[8,256,2048]{2,1,0:T(8,128)(2,1)} broadcast(bf16[256,2048]{1,0:T(8,128)(2,1)S(1)} %bitcast_multiply_fusion), dimensions={1,2} | broadcast | bytes 9437184 | tf_op jit(solution)/shard_map/stack | solution.py:19
  13.2 0.0 copy-start.1
  13.2 0.0 copy-start
  13.2 5.1 %all-to-all-start = ((bf16[8,256,2048]{2,1,0:T(8,128)(2,1)}), bf16[8,256,2048]{2,1,0:T(8,128)(2,1)}, u32[]{:S(2)}, u32[]{:S(2)}) async-start(bf16[8,256,2048]{2,1,0:T(8,128)(2,1)} %stack.3), calls=%async_computation | async-start | bytes 16777216 | tf_op jit(solution)/shard_map/all_to_all | solution.py:20
  18.3 0.0 all-gather.2.cloned.1.call-start
  18.3 0.0 copy-done.1
  18.3 0.1 copy.5
  18.4 0.3 mul.23
  18.8 0.0 copy-done
  18.8 1.1 bitcast_multiply_fusion.1
  19.9 0.0 all-gather.2.cloned.1.call-update
  19.9 0.0 reduce-scatter.2.cloned.1.call-start
  20.0 87.8 %all-gather.2.cloned.1.call-done = bf16[1024,2048]{1,0:T(8,128)(2,1)} async-done(((bf16[1024,512]{1,0:T(8,128)(2,1)}), bf16[1024,2048]{1,0:T(8,128)(2,1)}) %all-gather.2.cloned.1.call-update) | async-done | bytes 4194320 | tf_op jit(solution)/shard_map/all_gather | solution.py:22
  107.8 5.0 %all-to-all-done = bf16[8,256,2048]{2,1,0:T(8,128)(2,1)} async-done(((bf16[8,256,2048]{2,1,0:T(8,128)(2,1)}), bf16[8,256,2048]{2,1,0:T(8,128)(2,1)}, u32[]{:S(2)}, u32[]{:S(2)}) %all-to-all-start) | async-done | bytes 8388640 | tf_op jit(solution)/shard_map/all_to_all | solution.py:20
  112.8 14.4 %fusion = f32[1024,2048]{1,0:T(8,128)} fusion(bf16[1024,2048]{1,0:T(8,128)(2,1)} %all-gather.2.cloned.1.call-done, bf16[2048,2048]{1,0:T(8,128)(2,1)} %bitcast), kind=kOutput, calls=%fused_computation.2 | convolution fusion | flops 8589934592 | bytes 20971520 | tf_op jit(solution)/shard_map/dot_general | solution.py:21
  127.3 0.0 reduce-scatter.2.cloned.1.call-update
  127.3 183.2 %reduce-scatter.2.cloned.1.call-done = f32[128,2048]{1,0:T(8,128)} async-done(((f32[1024,2048]{1,0:T(8,128)}), f32[128,2048]{1,0:T(8,128)}) %reduce-scatter.2.cloned.1.call-update) | async-done | bytes 1048592 | tf_op jit(solution)/shard_map/reduce_scatter | solution.py:26
  (1 shorter events, 0.0 us)
Async XLA Ops:
  13.2 5.1 %copy-start.1 = (s32[8,4]{0,1:T(4,128)S(1)}, s32[8,4]{0,1:T(4,128)}, u32[]{:S(2)}) copy-start(s32[8,4]{0,1:T(4,128)} %param.5) | copy-start | bytes 388
  13.2 5.6 %copy-start = (bf16[1024,512]{1,0:T(8,128)(2,1)S(1)}, bf16[1024,512]{1,0:T(8,128)(2,1)}, u32[]{:S(2)}) copy-start(bf16[1024,512]{1,0:T(8,128)(2,1)} %param.4) | copy-start | bytes 3145732
  13.2 99.7 %all-to-all-start = ((bf16[8,256,2048]{2,1,0:T(8,128)(2,1)}), bf16[8,256,2048]{2,1,0:T(8,128)(2,1)}, u32[]{:S(2)}, u32[]{:S(2)}) async-start(bf16[8,256,2048]{2,1,0:T(8,128)(2,1)} %stack.3), calls=%async_computation | async-start | bytes 16777216 | tf_op jit(solution)/shard_map/all_to_all | solution.py:20
  18.3 89.5 %all-gather.2.cloned.1.call-start = ((), (), s32[]{:S(2)}) async-start(), calls=%async_computation.2 | async-start | bytes 5242880 | tf_op jit(solution)/shard_map/all_gather | solution.py:22
  19.9 290.5 %reduce-scatter.2.cloned.1.call-start = ((), (), s32[]{:S(2)}) async-start(), calls=%async_computation.3 | async-start | bytes 9437184 | tf_op jit(solution)/shard_map/reduce_scatter | solution.py:26
Sparse Core Ops, SparseCore 0:
  20.9 86.8 all-gather.1
  127.4 183.0 reduce-scatter.1
